TPU v7x, 256 devices: a whole 4x4x8 slice. The times are simulated.
256 devices in a mesh: cfg: 2 (over core), req: 8 (over z), seq: 16 (over y, x).
Axes of the slice: x: 4, y: 4, z: 8, core: 2. Of those that a mesh axis runs over, the one named last changes fastest.
Arguments:
- queries: bfloat16 [2, 8, 768, 1536], P('cfg', 'req', 'seq'), may hold values from -50 to 50
- text_cache: bfloat16 [2, 8, 2, 512, 1536], P('cfg', 'req'), may hold values from -6 to 6
- image_cache: bfloat16 [2, 8, 2, 768, 1536], P('cfg', 'req'), may hold values from -6 to 6
- fresh_kv: bfloat16 [2, 8, 2, 96, 1536], P('cfg', 'req', None, 'seq'), may hold values from -6 to 6
- fresh_slots: int32 [8, 96], P('req'), may hold values from 0 to 767, as said below
- fresh_pos: int32 [3, 8, 96], P(None, 'req', 'seq'), may hold values from 0 to 63
- image_len: int32 [8], replicated, may hold values from 384 to 768, as said below
- stream: bfloat16 [2, 8, 768, 3072], P('cfg', None, 'seq', 'req'), may hold values from -30 to 30
- modulation: float32 [2, 8, 4, 3072], replicated, may hold values from -4 to 4
- out_weight: bfloat16 [1536, 3072], P('seq', 'req'), may hold values from -0.15625 to 0.15625
- up_weight: bfloat16 [3072, 12288], P('seq', 'req'), may hold values from -0.109375 to 0.109375
- down_weight: bfloat16 [12288, 3072], P('req', 'seq'), may hold values from -0.0546875 to 0.0546875
- final_weight: bfloat16 [3072, 64], replicated, may hold values from -0.109375 to 0.109375
- latent: float32 [8, 384, 128], P('req', 'seq', 'cfg'), may hold values from -6 to 6
- step_index: int32 [1], replicated, may hold values from 0 to 27
Outputs:
- latent_next: float32 [8, 384, 128], P('req', 'seq', 'cfg')
- denoised: float32 [8, 384, 128], P('req', 'seq', 'cfg')
Inputs may be any that keep to these rules, and one draw needn't show every extreme that they name: `fresh_slots`: columns k * 6 to (k + 1) * 6 - 1 of a row hold distinct slots from k * 48 to (k + 1) * 48 - 1. `image_len`: some request has exactly 768 image tokens and some other exactly 384.
All inputs are finite; a program needn't handle non-finite values.
Results may differ from a plain program's by a relative error of at most 0.0095.
Values may be sent and summed in bfloat16 or wider, within the bound.
A program may use at most 128 MiB of HBM per device.

v0:
```python
import math
import jax
import jax.numpy as jnp
from jax import lax
from jax.sharding import PartitionSpec as P

STEPS = 28
GUIDANCE = 3.0
SHIFT = 3.0
SCALE = 1.0 / math.sqrt(128.0)
EPSILON = 1e-06


def swapped(block, axis, stride):
    count = lax.axis_size(axis)
    route = []
    for low in range(count):
        high = low | 1 << stride
        if high != low and high < count:
            route += [(low, high), (high, low)]
    return lax.ppermute(block, axis, route)


def rope_angles(positions):
    columns = []
    for component, axis_span in ((0, 16), (1, 56), (2, 56)):
        pair_ids = jnp.arange(axis_span // 2, dtype=jnp.float32)
        frequency = jnp.exp(-(2.0 * pair_ids / axis_span) * math.log(10000.0))
        columns.append(positions[component].astype(jnp.float32)[:, None] * frequency[None, :])
    return jnp.concatenate(columns, axis=1)


def rotate(key_rows, angles):
    row_total = key_rows.shape[0]
    paired = key_rows.reshape(row_total, -1, 64, 2)
    cosine = jnp.cos(angles)[:, None, :]
    sine = jnp.sin(angles)[:, None, :]
    first = cosine * paired[..., 0] - sine * paired[..., 1]
    second = sine * paired[..., 0] + cosine * paired[..., 1]
    return jnp.stack([first, second], axis=-1).reshape(row_total, -1)


def noise_level(index):
    fraction = 1.0 - index.astype(jnp.float32) / STEPS
    return SHIFT * fraction / (SHIFT * fraction + 1.0 - fraction)


def head_scores(query_heads, key_rows):
    key_heads = key_rows.reshape(key_rows.shape[0], -1, 128)
    return (
        jnp.einsum("qhd,khd->hqk", query_heads, key_heads, preferred_element_type=jnp.float32)
        * SCALE
    )


def head_mix(weights, value_rows):
    value_heads = value_rows.reshape(value_rows.shape[0], -1, 128)
    return jnp.einsum("hqk,khd->qhd", weights, value_heads, preferred_element_type=jnp.float32)


def per_device(
    queries,
    text_cache,
    image_cache,
    fresh_kv,
    fresh_slots,
    fresh_pos,
    image_len,
    stream,
    modulation,
    out_weight,
    up_weight,
    down_weight,
    final_weight,
    latent,
    step_index,
):
    cfg_id = lax.axis_index("cfg")
    req_id = lax.axis_index("req")
    seq_id = lax.axis_index("seq")
    query_rows = queries[0, 0]
    row_count = query_rows.shape[0]
    query_heads = query_rows.reshape(row_count, -1, 128)
    text_kv = text_cache[0, 0]
    image_kv = image_cache[0, 0]
    angles = rope_angles(fresh_pos[:, 0, :])
    fresh_keys = rotate(fresh_kv[0, 0, 0].astype(jnp.float32), angles).astype(jnp.bfloat16)
    fresh_pair = jnp.stack([fresh_keys, fresh_kv[0, 0, 1]], axis=0)
    all_fresh, proj_cols, up_cols, down_rows = (
        lax.all_gather(fresh_pair, "seq", axis=1, tiled=True),
        lax.all_gather(out_weight, "seq", axis=0, tiled=True),
        lax.all_gather(up_weight, "seq", axis=0, tiled=True),
        lax.all_gather(down_weight, "seq", axis=1, tiled=True),
    )
    image_kv = image_kv.at[:, fresh_slots[0], :].set(all_fresh)
    length = lax.dynamic_index_in_dim(image_len, req_id, 0, keepdims=False)
    image_total = image_kv.shape[1]
    text_scores = head_scores(query_heads, text_kv[0])
    text_best = jnp.max(text_scores, axis=-1, keepdims=True)
    live_keys = (jnp.arange(image_total) < length)[None, None, :]
    image_scores = jnp.where(live_keys, head_scores(query_heads, image_kv[0]), -jnp.inf)
    row_max = jnp.maximum(text_best, jnp.max(image_scores, axis=-1, keepdims=True))
    text_probs = jnp.exp(text_scores - row_max)
    image_probs = jnp.exp(image_scores - row_max)
    total = jnp.sum(text_probs, axis=-1) + jnp.sum(image_probs, axis=-1)
    mixed = head_mix(text_probs.astype(jnp.bfloat16), text_kv[1]) + head_mix(
        image_probs.astype(jnp.bfloat16), image_kv[1]
    )
    attended = (
        (mixed / jnp.transpose(total)[:, :, None]).reshape(row_count, -1).astype(jnp.bfloat16)
    )
    projected = jnp.dot(
        lax.all_gather(attended, "req", axis=0, tiled=True),
        proj_cols,
        preferred_element_type=jnp.float32,
    )
    requests = stream.shape[1]
    col_count = stream.shape[3]
    mod_half = lax.dynamic_index_in_dim(modulation, cfg_id, 0, keepdims=False)
    gate_cols = lax.dynamic_slice_in_dim(mod_half[:, 0, :], req_id * col_count, col_count, 1)
    residual = (
        stream[0].astype(jnp.float32)
        + gate_cols[:, None, :] * projected.reshape(requests, row_count, col_count)
    ).astype(jnp.bfloat16)
    full_rows = lax.all_gather(
        residual.reshape(requests * row_count, col_count), "req", axis=1, tiled=True
    )
    wide = full_rows.reshape(requests, row_count, -1).astype(jnp.float32)
    average = jnp.mean(wide, axis=-1, keepdims=True)
    centered = wide - average
    spread = jnp.mean(centered * centered, axis=-1, keepdims=True)
    normed = (
        centered * lax.rsqrt(spread + EPSILON) * (1.0 + mod_half[:, 2][:, None, :])
        + mod_half[:, 1][:, None, :]
    )
    normed = normed.astype(jnp.bfloat16).reshape(requests * row_count, -1)

    def rows_product(left_rows, right):
        return jnp.dot(left_rows, right, preferred_element_type=jnp.float32)

    pre_act = rows_product(normed, up_cols)
    activated = jax.nn.gelu(pre_act, approximate=True).astype(jnp.bfloat16)
    mlp_rows = lax.psum_scatter(
        rows_product(activated, down_rows).astype(jnp.bfloat16),
        "req",
        scatter_dimension=0,
        tiled=True,
    ).astype(jnp.float32)
    own_rows = lax.dynamic_slice_in_dim(full_rows, req_id * row_count, row_count, 0)
    gate_two = lax.dynamic_index_in_dim(mod_half[:, 3, :], req_id, 0, keepdims=False)
    block_out = (own_rows.astype(jnp.float32) + gate_two[None, :] * mlp_rows).astype(jnp.bfloat16)
    velocity = jnp.dot(block_out, final_weight, preferred_element_type=jnp.float32).reshape(
        row_count // 2, -1
    )
    lane_count = velocity.shape[1]
    half_lanes = lane_count // 2
    outgoing = lax.dynamic_slice_in_dim(velocity, (1 - cfg_id) * half_lanes, half_lanes, 1)
    own_part = lax.dynamic_slice_in_dim(velocity, cfg_id * half_lanes, half_lanes, 1)
    partner = swapped(outgoing, "cfg", 0)
    cond_part = jnp.where(cfg_id == 0, own_part, partner)
    uncond_part = jnp.where(cfg_id == 0, partner, own_part)
    guided = uncond_part + GUIDANCE * (cond_part - uncond_part)
    level_now = noise_level(step_index[0])
    level_next = noise_level(step_index[0] + 1)
    token_ids = (
        seq_id * row_count
        + 2 * jnp.arange(row_count // 2, dtype=jnp.int32)[:, None]
        + cfg_id
        + jnp.zeros((1, half_lanes), jnp.int32)
    )
    valid = token_ids < length
    current = latent[0]
    latent_next = jnp.where(valid, current + (level_next - level_now) * guided, current)
    denoised = jnp.where(valid, current - level_now * guided, current)
    return (latent_next[None], denoised[None])


def solution(mesh):
    in_specs = (
        P("cfg", "req", "seq", None),
        P("cfg", "req", None, None, None),
        P("cfg", "req", None, None, None),
        P("cfg", "req", None, "seq", None),
        P("req", None),
        P(None, "req", "seq"),
        P(),
        P("cfg", None, "seq", "req"),
        P(),
        P("seq", "req"),
        P("seq", "req"),
        P("req", "seq"),
        P(),
        P("req", "seq", "cfg"),
        P(),
    )
    out_specs = (P("req", "seq", "cfg"), P("req", "seq", "cfg"))
    return jax.shard_map(
        per_device, mesh=mesh, in_specs=in_specs, out_specs=out_specs, check_vma=False
    )
```

profile of v0, /device:TPU:1, one launch (start us, length us, event | category | flops | bytes accessed | tf_op | source)
XLA Modules:
  0.0 484.3 jit_solution(10954910353682535081)
XLA Ops:
  7.3 0.8 convert_bitcast_fusion.2
  8.5 0.9 fusion.58
  9.7 1.0 multiply_subtract_fusion
  10.7 0.4 copy.66
  11.1 0.4 copy.67
  11.6 0.4 copy.68
  12.1 0.3 copy.70
  12.5 20.3 %all_gather.18 = bf16[2,96,1536]{2,0,1:T(2,128)(2,1)S(1)} all-gather(bf16[2,6,1536]{2,0,1:T(2,128)(2,1)S(1)} %pad_maximum_fusion.1), channel_id=1, replica_groups=mesh['cfg'=2,'req'=8,'seq'=16] {'seq'}, dimensions={1}, use_global_device_ids=true | all-gather | bytes 626688 | tf_op jit(solution)/shard_map/all_gather | solution.py:90
  32.8 9.4 %copy.107 = bf16[1,1,2,768,1536]{4,2,3,1,0:T(2,128)(2,1)} copy(bf16[1,1,2,768,1536]{4,3,2,1,0:T(8,128)(2,1)} %param.17) | data formatting | bytes 9437184 | tf_op args[2]
  42.2 11.7 %scatter_fusion = bf16[2,768,1536]{2,0,1:T(2,128)(2,1)} fusion(bf16[2,768,1536]{2,0,1:T(2,128)(2,1)} %bitcast.99, s32[96]{0:T(128)S(1)} %fusion.46, bf16[96,2,1536]{2,1,0:T(2,128)(2,1)S(1)} %bitcast.106), kind=kCustom, calls=%fused_computation | custom fusion | bytes 1769856 | tf_op jit(solution)/shard_map/scatter | solution.py:95
  53.9 10.7 %fusion.55 = (bf16[1,768,1536]{2,0,1:T(2,128)(2,1)}, bf16[1,768,1536]{2,0,1:T(2,128)(2,1)}) fusion(bf16[2,768,1536]{2,0,1:T(2,128)(2,1)} %scatter_fusion), kind=kLoop, calls=%fused_computation.100 | loop fusion | bytes 9437184 | tf_op jit(solution)/shard_map/slice | solution.py:107
  64.6 11.7 %copy.72 = bf16[1,768,1536]{1,2,0:T(8,128)(2,1)} copy(bf16[1,768,1536]{2,0,1:T(2,128)(2,1)} %get-tuple-element.3) | data formatting | bytes 4718592 | tf_op jit(solution)/shard_map/slice | solution.py:101
  76.4 0.6 dynamic_slice.24
  76.9 0.6 iota_compare_fusion
  77.6 0.8 reshape_squeeze.15
  78.4 3.7 fusion.56
  82.2 1.7 copy.87
  83.9 1.5 fusion.59
  85.7 0.6 bitcast_reduce_fusion
  86.3 1.3 copy-done.4
  87.6 1.2 fusion.15
  88.7 1.0 fusion.28
  89.7 1.7 copy.90
  91.4 1.5 convolution_bitcast_fusion.1
  92.9 11.8 %copy.77 = bf16[1,768,1536]{1,2,0:T(8,128)(2,1)} copy(bf16[1,768,1536]{2,0,1:T(2,128)(2,1)} %get-tuple-element.2) | data formatting | bytes 4718592 | tf_op jit(solution)/shard_map/slice | solution.py:107
  104.8 2.7 fusion.27
  107.5 0.7 copy.108
  108.2 0.7 all-gather.8.cloned.1.call-update
  109.3 0.9 fusion.57
  110.2 39.1 %all-gather.6.cloned.1.call-done = bf16[384,1536]{1,0:T(8,128)(2,1)} async-done(((bf16[48,1536]{1,0:T(8,128)(2,1)}), bf16[384,1536]{1,0:T(8,128)(2,1)}) %all-gather.6.cloned.1.call-update) | async-done | bytes 1179664 | tf_op jit(solution)/shard_map/all_gather | solution.py:113
  149.3 52.0 %all-gather.8.cloned.1.call-done = bf16[1536,384]{1,0:T(8,128)(2,1)} async-done(((bf16[96,384]{1,0:T(8,128)(2,1)}), bf16[1536,384]{1,0:T(8,128)(2,1)}) %all-gather.8.cloned.1.call-update) | async-done | bytes 1179664 | tf_op jit(solution)/shard_map/all_gather | solution.py:91
  201.4 3.1 fusion.18
  204.6 0.5 all-gather.12.cloned.1.call-update
  205.2 0.5 all-gather.14.cloned.1.call-update
  205.8 38.7 %all-gather.10.cloned.1.call-done = bf16[384,3072]{1,0:T(8,128)(2,1)} async-done(((bf16[384,384]{1,0:T(8,128)(2,1)}), bf16[384,3072]{1,0:T(8,128)(2,1)}) %all-gather.10.cloned.1.call-update) | async-done | bytes 2359312 | tf_op jit(solution)/shard_map/all_gather | solution.py:125
  244.5 2.2 convert_reduce_fusion
  246.9 0.8 fusion.2
  247.6 2.6 fusion.5
  250.3 78.9 %all-gather.12.cloned.1.call-done = bf16[3072,1536]{1,0:T(8,128)(2,1)} async-done(((bf16[192,1536]{1,0:T(8,128)(2,1)}), bf16[3072,1536]{1,0:T(8,128)(2,1)}) %all-gather.12.cloned.1.call-update) | async-done | bytes 9437200 | tf_op jit(solution)/shard_map/all_gather | solution.py:92
  329.2 82.8 %all-gather.14.cloned.1.call-done = bf16[1536,3072]{0,1:T(8,128)(2,1)} async-done(((bf16[1536,192]{0,1:T(8,128)(2,1)}), bf16[1536,3072]{0,1:T(8,128)(2,1)}) %all-gather.14.cloned.1.call-update) | async-done | bytes 9437200 | tf_op jit(solution)/shard_map/all_gather | solution.py:93
  412.0 16.2 %convolution_convert_fusion = bf16[384,3072]{1,0:T(8,128)(2,1)} fusion(bf16[1536,3072]{0,1:T(8,128)(2,1)} %all-gather.14.cloned.1.call-done, bf16[384,3072]{1,0:T(8,128)(2,1)} %fusion.5, bf16[3072,1536]{1,0:T(8,128)(2,1)} %all-gather.12.cloned.1.call-done), kind=kOutput, calls=%fused_computation.10 | convolution fusion | flops 7254245376 | bytes 23592960 | tf_op jit(solution)/shard_map/dot_general | solution.py:139
  428.1 0.8 constant_dynamic-slice_fusion.1
  428.9 37.9 %reduce-scatter.2.cloned.1.call-done = bf16[48,3072]{1,0:T(8,128)(2,1)} async-done(((bf16[384,3072]{1,0:T(8,128)(2,1)}), bf16[48,3072]{1,0:T(8,128)(2,1)}) %reduce-scatter.2.cloned.1.call-update) | async-done | bytes 294928 | tf_op jit(solution)/shard_map/reduce_scatter | solution.py:143
  466.8 1.8 fusion.37
  468.6 0.8 reshape.245
  469.5 5.2 %collective-permute-start = (f32[24,64]{1,0:T(8,128)S(1)}, f32[24,64]{1,0:T(8,128)S(1)}, u32[]{:S(2)}, u32[]{:S(2)}) collective-permute-start(f32[24,64]{1,0:T(8,128)S(1)} %constant_dynamic-slice_fusion), channel_id=1, source_target_pairs={{0,128},{128,0},{1,129},{129,1},{2,130},{130,2},{3,131},{131,3},{4... | collective-permute-start | bytes 18440 | tf_op jit(solution)/shard_map/ppermute | solution.py:21
  474.7 0.6 add_compare_fusion
  476.0 1.4 fusion.44
  (65 shorter events, 2.2 us)
Async XLA Ops:
  7.2 102.0 %copy-start = (f32[2,8,4,3072]{3,2,1,0:T(4,128)S(1)}, f32[2,8,4,3072]{3,2,1,0:T(4,128)}, u32[]{:S(2)}) copy-start(f32[2,8,4,3072]{3,2,1,0:T(4,128)} %param.23) | copy-start | bytes 2359300
  7.2 142.1 %all-gather.6.cloned.1.call-start = ((), (), s32[]{:S(2)}) async-start(), calls=%async_computation.1 | async-start | bytes 1327104 | tf_op jit(solution)/shard_map/all_gather | solution.py:113
  32.8 9.4 %copy-start.14 = (s32[1,96]{1,0:T(1,128)S(1)}, s32[1,96]{1,0:T(1,128)}, u32[]{:S(2)}) copy-start(s32[1,96]{1,0:T(1,128)} %param.19) | copy-start | bytes 1156
  64.6 11.8 %copy-start.15 = (s32[8]{0:T(128)S(1)}, s32[8]{0:T(128)}, u32[]{:S(2)}) copy-start(s32[8]{0:T(128)} %param.21) | copy-start | bytes 100
  64.6 13.0 %copy-start.10 = (bf16[1,1,48,1536]{3,2,1,0:T(8,128)(2,1)S(1)}, bf16[1,1,48,1536]{3,2,1,0:T(8,128)(2,1)}, u32[]{:S(2)}) copy-start(bf16[1,1,48,1536]{3,2,1,0:T(8,128)(2,1)} %param.15) | copy-start | bytes 442372
  77.6 7.9 %copy-start.12 = (pred[768]{0:T(1024)(128)(4,1)}, pred[768]{0:T(1024)(128)(4,1)S(1)}, u32[]{:S(2)}) copy-start(pred[768]{0:T(1024)(128)(4,1)S(1)} %iota_compare_fusion) | copy-start | bytes 2308
  83.9 1.8 copy-start.3
  83.9 1.8 copy-start.6
  86.3 1.3 copy-start.4
  92.9 11.9 %copy-start.11 = (f32[12,48]{1,0:T(8,128)S(1)}, f32[12,48]{1,0:T(8,128)}, u32[]{:S(2)}) copy-start(f32[12,48]{1,0:T(8,128)} %fusion.28) | copy-start | bytes 6916
  92.9 11.9 %copy-start.5 = (f32[12,768,48]{1,2,0:T(8,128)S(1)}, f32[12,768,48]{1,2,0:T(8,128)}, u32[]{:S(2)}) copy-start(f32[12,768,48]{1,2,0:T(8,128)} %copy-done.4) | copy-start | bytes 5308420
  92.9 11.9 %copy-start.9 = (f32[48,12,128]{2,0,1:T(8,128)S(1)}, f32[48,12,128]{2,0,1:T(8,128)}, u32[]{:S(2)}) copy-start(f32[48,12,128]{2,0,1:T(8,128)} %convolution_bitcast_fusion.1) | copy-start | bytes 884740
  92.9 11.9 %copy-start.13 = (pred[768]{0:T(1024)(128)(4,1)S(1)}, pred[768]{0:T(1024)(128)(4,1)}, u32[]{:S(2)}) copy-start(pred[768]{0:T(1024)(128)(4,1)} %copy-done.12) | copy-start | bytes 2308
  107.5 93.9 %copy-start.8 = (bf16[1,8,48,384]{3,2,1,0:T(8,128)(2,1)S(1)}, bf16[1,8,48,384]{3,2,1,0:T(8,128)(2,1)}, u32[]{:S(2)}) copy-start(bf16[1,8,48,384]{3,2,1,0:T(8,128)(2,1)} %param.22) | copy-start | bytes 884740
  108.2 93.2 %all-gather.8.cloned.1.call-start = ((), (), s32[]{:S(2)}) async-start(), calls=%async_computation.2 | async-start | bytes 1253376 | tf_op jit(solution)/shard_map/all_gather | solution.py:91
  108.9 135.6 %all-gather.10.cloned.1.call-start = ((), (), s32[]{:S(2)}) async-start(), calls=%async_computation.3 | async-start | bytes 2654208 | tf_op jit(solution)/shard_map/all_gather | solution.py:125
  204.6 124.6 %all-gather.12.cloned.1.call-start = ((), (), s32[]{:S(2)}) async-start(), calls=%async_computation.4 | async-start | bytes 10027008 | tf_op jit(solution)/shard_map/all_gather | solution.py:92
  205.1 206.8 %all-gather.14.cloned.1.call-start = ((), (), s32[]{:S(2)}) async-start(), calls=%async_computation.5 | async-start | bytes 10027008 | tf_op jit(solution)/shard_map/all_gather | solution.py:93
  205.7 261.1 %reduce-scatter.2.cloned.1.call-start = ((), (), s32[]{:S(2)}) async-start(), calls=%async_computation.6 | async-start | bytes 2654208 | tf_op jit(solution)/shard_map/reduce_scatter | solution.py:143
  244.5 2.4 copy-start.2
  412.0 65.5 %copy-start.1 = (f32[2,8,4,3072]{3,2,1,0:T(4,128)S(1)}, f32[2,8,4,3072]{3,2,1,0:T(4,128)}, u32[]{:S(2)}) copy-start(f32[2,8,4,3072]{3,2,1,0:T(4,128)} %param.23) | copy-start | bytes 2359300
  428.1 38.7 %copy-start.7 = (bf16[3072,64]{0,1:T(8,128)(2,1)S(1)}, bf16[3072,64]{0,1:T(8,128)(2,1)}, u32[]{:S(2)}) copy-start(bf16[3072,64]{0,1:T(8,128)(2,1)} %param.27) | copy-start | bytes 1179652
  469.5 6.5 %collective-permute-start = (f32[24,64]{1,0:T(8,128)S(1)}, f32[24,64]{1,0:T(8,128)S(1)}, u32[]{:S(2)}, u32[]{:S(2)}) collective-permute-start(f32[24,64]{1,0:T(8,128)S(1)} %constant_dynamic-slice_fusion), channel_id=1, source_target_pairs={{0,128},{128,0},{1,129},{129,1},{2,130},{130,2},{3,131},{131,3},{4... | collective-permute-start | bytes 18440 | tf_op jit(solution)/shard_map/ppermute | solution.py:21
Sparse Core Ops, SparseCore 0:
  108.3 40.9 all-gather.5
  151.8 49.5 all-gather.7
  204.7 39.7 all-gather.9
  246.8 82.3 all-gather.11
  331.5 80.4 all-gather.13
  428.3 38.5 reduce-scatter.1
where the time goes:
time: 486 us; the launch traced here: 484 us
  waiting for transfers between devices  331 us (68%)
  local copies, waits for them, and re-layouts  71.1 us (15%)
  matrix products  27.3 us (6%)
  blocking collectives  20.3 us (4%)
  between operations  15.2 us (3%)
  other arithmetic  13.6 us (3%)
  starting transfers between devices  5.61 us (1%)
    all_gather x1, waiting for transfers between devices, per_device(): lax.all_gather(down_weight, 'seq', axis=1, tiled=True)  82.8 us
    all_gather x1, waiting for transfers between devices, per_device(): lax.all_gather(up_weight, 'seq', axis=0, tiled=True)  78.9 us
    all_gather x1, waiting for transfers between devices, per_device(): lax.all_gather(out_weight, 'seq', axis=0, tiled=True)  52 us
    all_gather x1, waiting for transfers between devices, per_device(): lax.all_gather(attended, 'req', axis=0, tiled=True)  39.1 us
    all_gather x1, waiting for transfers between devices, per_device(): lax.all_gather(residual.reshape(requests * row_count, col_count), 'req',...  38.7 us
    reduce_scatter x1, waiting for transfers between devices, per_device(): lax.psum_scatter(rows_product(activated, down_rows).astype(jnp.bfloat16),...  37.9 us
    slice x2, local copies, waits for them, and re-layouts, per_device(): image_kv[1]  22.5 us
    all_gather x1, blocking collectives, per_device(): lax.all_gather(fresh_pair, 'seq', axis=1, tiled=True)  20.3 us
  transfers between devices with their start and end apart: 7, of which 6 were waited for; matrix products, arithmetic and copies ran while one was open for 2% of the time, Pallas kernels for 0%

commit v1 on v0

--- a/solution.py
+++ b/solution.py
@@ -122,8 +122,14 @@
         stream[0].astype(jnp.float32)
         + gate_cols[:, None, :] * projected.reshape(requests, row_count, col_count)
     ).astype(jnp.bfloat16)
-    full_rows = lax.all_gather(
-        residual.reshape(requests * row_count, col_count), "req", axis=1, tiled=True
+    full_rows = jnp.concatenate(
+        lax.all_to_all(
+            jnp.stack([residual.reshape(requests * row_count, col_count)] * lax.axis_size("req")),
+            "req",
+            0,
+            0,
+        ),
+        axis=1,
     )
     wide = full_rows.reshape(requests, row_count, -1).astype(jnp.float32)
     average = jnp.mean(wide, axis=-1, keepdims=True)

time: 486 us -> 442 us (0.909)
  waiting for transfers between devices: 331 us -> 263 us
  local copies, waits for them, and re-layouts: 71.1 us -> 92.8 us
  starting transfers between devices: 5.61 us -> 11.9 us
    all_gather x1, waiting for transfers between devices: 82.8 us -> 14 us  [per_device(): lax.all_gather(down_weight, 'seq', axis=1, tiled=True)]
    all_to_all x0 -> x1, waiting for transfers between devices: none -> 39.5 us  [per_device(): lax.all_to_all(jnp.stack([residual.reshape(requests * row_count, col_coun...]
    all_gather x1 -> x0, waiting for transfers between devices: 38.7 us -> none  [per_device(): lax.all_gather(residual.reshape(requests * row_count, col_count), 'req',...]
    mul x0 -> x2, local copies, waits for them, and re-layouts: none -> 8.99 us  [per_device(): centered * lax.rsqrt(spread + EPSILON) * (1.0 + mod_half[:, 2][:, None, :])]
    add x0 -> x2, local copies, waits for them, and re-layouts: none -> 8.77 us  [per_device(): centered * lax.rsqrt(spread + EPSILON) * (1.0 + mod_half[:, 2][:, None, :])]
    all_to_all x0 -> x1, starting transfers between devices: none -> 6.73 us  [per_device(): lax.all_to_all(jnp.stack([residual.reshape(requests * row_count, col_coun...]
    unnamed x38 -> x35, local copies, waits for them, and re-layouts: 14.6 us -> 15.8 us
  transfers between devices with their start and end apart: 7 -> 7, of which waited for: 6 -> 6; matrix products, arithmetic and copies ran while one was open for 2% -> 6% of each run, Pallas kernels for 0% -> 0%
where the time goes in v1:
time: 442 us; the launch traced here: 441 us
  waiting for transfers between devices  263 us (60%)
  local copies, waits for them, and re-layouts  92.8 us (21%)
  matrix products  28.5 us (6%)
  blocking collectives  20.3 us (5%)
  between operations  14.9 us (3%)
  starting transfers between devices  11.9 us (3%)
  other arithmetic  9.04 us (2%)
    all_gather x1, waiting for transfers between devices, per_device(): lax.all_gather(up_weight, 'seq', axis=0, tiled=True)  82.8 us
    all_gather x1, waiting for transfers between devices, per_device(): lax.all_gather(out_weight, 'seq', axis=0, tiled=True)  52 us
    all_to_all x1, waiting for transfers between devices, per_device(): lax.all_to_all(jnp.stack([residual.reshape(requests * row_count, col_coun...  39.5 us
    all_gather x1, waiting for transfers between devices, per_device(): lax.all_gather(attended, 'req', axis=0, tiled=True)  38.1 us
    reduce_scatter x1, waiting for transfers between devices, per_device(): lax.psum_scatter(rows_product(activated, down_rows).astype(jnp.bfloat16),...  35.3 us
    slice x2, local copies, waits for them, and re-layouts, per_device(): image_kv[1]  22.5 us
    all_gather x1, blocking collectives, per_device(): lax.all_gather(fresh_pair, 'seq', axis=1, tiled=True)  20.3 us
    dot_general x1, matrix products, rows_product(): return jnp.dot(left_rows, right, preferred_element_type=jnp.float32)  18.7 us
  transfers between devices with their start and end apart: 7, of which 6 were waited for; matrix products, arithmetic and copies ran while one was open for 6% of the time, Pallas kernels for 0%

profile of v1, /device:TPU:1, one launch (start us, length us, event | category | flops | bytes accessed | tf_op | source)
XLA Modules:
  0.0 440.8 jit_solution(15359245102516222647)
XLA Ops:
  7.3 0.8 convert_bitcast_fusion.2
  8.5 0.9 fusion.47
  9.7 1.0 multiply_subtract_fusion
  12.5 20.3 %all_gather.15 = bf16[2,96,1536]{2,0,1:T(2,128)(2,1)S(1)} all-gather(bf16[2,6,1536]{2,0,1:T(2,128)(2,1)S(1)} %pad_maximum_fusion.1), channel_id=1, replica_groups=mesh['cfg'=2,'req'=8,'seq'=16] {'seq'}, dimensions={1}, use_global_device_ids=true | all-gather | bytes 626688 | tf_op jit(solution)/shard_map/all_gather | solution.py:90
  32.8 9.4 %copy.135 = bf16[1,1,2,768,1536]{4,2,3,1,0:T(2,128)(2,1)} copy(bf16[1,1,2,768,1536]{4,3,2,1,0:T(8,128)(2,1)} %param.17) | data formatting | bytes 9437184 | tf_op args[2]
  42.3 11.7 %scatter_fusion = bf16[2,768,1536]{2,0,1:T(2,128)(2,1)} fusion(bf16[2,768,1536]{2,0,1:T(2,128)(2,1)} %bitcast.98, s32[96]{0:T(128)S(1)} %fusion.39, bf16[96,2,1536]{2,1,0:T(2,128)(2,1)S(1)} %bitcast.109), kind=kCustom, calls=%fused_computation | custom fusion | bytes 1769856 | tf_op jit(solution)/shard_map/scatter | solution.py:95
  53.9 10.7 %fusion.44 = (bf16[1,768,1536]{2,0,1:T(2,128)(2,1)}, bf16[1,768,1536]{2,0,1:T(2,128)(2,1)}) fusion(bf16[2,768,1536]{2,0,1:T(2,128)(2,1)} %scatter_fusion), kind=kLoop, calls=%fused_computation.91 | loop fusion | bytes 9437184 | tf_op jit(solution)/shard_map/slice | solution.py:107
  64.6 11.7 %copy.100 = bf16[1,768,1536]{1,2,0:T(8,128)(2,1)} copy(bf16[1,768,1536]{2,0,1:T(2,128)(2,1)} %get-tuple-element.3) | data formatting | bytes 4718592 | tf_op jit(solution)/shard_map/slice | solution.py:101
  76.4 0.7 dynamic_slice.24
  77.0 0.7 iota_compare_fusion
  77.8 0.8 reshape_squeeze.15
  78.6 3.7 fusion.45
  82.3 1.7 copy.116
  84.1 1.5 fusion.48
  85.8 0.6 bitcast_reduce_fusion
  86.4 1.3 copy-done.3
  87.7 1.2 fusion.14
  88.9 1.0 fusion.22
  89.9 1.7 copy.119
  91.6 1.4 convolution_bitcast_fusion.1
  93.0 11.8 %copy.105 = bf16[1,768,1536]{1,2,0:T(8,128)(2,1)} copy(bf16[1,768,1536]{2,0,1:T(2,128)(2,1)} %get-tuple-element.2) | data formatting | bytes 4718592 | tf_op jit(solution)/shard_map/slice | solution.py:107
  104.9 2.7 fusion.21
  107.6 0.7 copy.137
  108.3 0.7 all-gather.7.cloned.1.call-update
  109.1 0.7 all-gather.11.cloned.1.call-update
  110.6 0.7 fusion.46
  111.3 38.1 %all-gather.5.cloned.1.call-done = bf16[384,1536]{1,0:T(8,128)(2,1)} async-done(((bf16[48,1536]{1,0:T(8,128)(2,1)}), bf16[384,1536]{1,0:T(8,128)(2,1)}) %all-gather.5.cloned.1.call-update) | async-done | bytes 1179664 | tf_op jit(solution)/shard_map/all_gather | solution.py:113
  149.4 52.0 %all-gather.7.cloned.1.call-done = bf16[1536,384]{1,0:T(8,128)(2,1)} async-done(((bf16[96,384]{1,0:T(8,128)(2,1)}), bf16[1536,384]{1,0:T(8,128)(2,1)}) %all-gather.7.cloned.1.call-update) | async-done | bytes 1179664 | tf_op jit(solution)/shard_map/all_gather | solution.py:91
  201.5 2.4 fusion.17
  204.1 1.6 stack.15
  205.7 6.7 %all-to-all-start = ((bf16[8,384,384]{1,2,0:T(8,128)(2,1)}), bf16[8,384,384]{1,2,0:T(8,128)(2,1)S(1)}, u32[]{:S(2)}, u32[]{:S(2)}) async-start(bf16[8,384,384]{1,2,0:T(8,128)(2,1)} %stack.15), calls=%async_computation | async-start | bytes 4718592 | tf_op jit(solution)/shard_map/all_to_all | solution.py:126
  212.5 2.8 mul.272
  215.3 6.2 %copy.110 = f32[384,3072]{0,1:T(8,128)} copy(f32[384,3072]{1,0:T(8,128)} %bitcast.101) | data formatting | bytes 9437184 | tf_op jit(solution)/shard_map/mul | solution.py:139
  221.5 2.7 add.165
  224.2 6.1 %copy.111 = f32[384,3072]{0,1:T(8,128)} copy(f32[384,3072]{1,0:T(8,128)} %bitcast.102) | data formatting | bytes 9437184 | tf_op jit(solution)/shard_map/add | solution.py:139
  230.3 39.5 %all-to-all-done = bf16[8,384,384]{1,2,0:T(8,128)(2,1)S(1)} async-done(((bf16[8,384,384]{1,2,0:T(8,128)(2,1)}), bf16[8,384,384]{1,2,0:T(8,128)(2,1)S(1)}, u32[]{:S(2)}, u32[]{:S(2)}) %all-to-all-start) | async-done | bytes 2359328 | tf_op jit(solution)/shard_map/all_to_all | solution.py:126
  270.2 0.7 fusion.1
  270.9 14.0 %all-gather.11.cloned.1.call-done = bf16[1536,3072]{0,1:T(8,128)(2,1)} async-done(((bf16[1536,192]{0,1:T(8,128)(2,1)}), bf16[1536,3072]{0,1:T(8,128)(2,1)}) %all-gather.11.cloned.1.call-update) | async-done | bytes 9437200 | tf_op jit(solution)/shard_map/all_gather | solution.py:93
  284.9 82.8 %all-gather.9.cloned.1.call-done = bf16[3072,1536]{1,0:T(8,128)(2,1)} async-done(((bf16[192,1536]{1,0:T(8,128)(2,1)}), bf16[3072,1536]{1,0:T(8,128)(2,1)}) %all-gather.9.cloned.1.call-update) | async-done | bytes 9437200 | tf_op jit(solution)/shard_map/all_gather | solution.py:92
  367.7 18.7 %convolution_convert_fusion = bf16[384,3072]{1,0:T(8,128)(2,1)} fusion(bf16[1536,3072]{0,1:T(8,128)(2,1)} %all-gather.11.cloned.1.call-done, bf16[3072,1536]{1,0:T(8,128)(2,1)} %all-gather.9.cloned.1.call-done, f32[384,3072]{0,1:T(8,128)} %copy.111, f32[384,3072]{0,1:T(8,128)} %copy.110, bf16[384,3072]{0,1:T(8,128)(2,1)S(1)} %bitcast.99, ...), kind=kOutput, calls=%fused_computation.7 | convolution fusion | flops 7261323264 | bytes 33033216 | tf_op jit(solution)/shard_map/dot_general | solution.py:145
  386.4 1.0 constant_dynamic-slice_fusion.1
  387.4 1.2 constant_dynamic-slice_fusion.2
  388.6 1.4 copy.120
  390.0 35.3 %reduce-scatter.2.cloned.1.call-done = bf16[48,3072]{1,0:T(8,128)(2,1)} async-done(((bf16[384,3072]{1,0:T(8,128)(2,1)}), bf16[48,3072]{1,0:T(8,128)(2,1)}) %reduce-scatter.2.cloned.1.call-update) | async-done | bytes 294928 | tf_op jit(solution)/shard_map/reduce_scatter | solution.py:149
  425.3 1.2 fusion.31
  426.6 4.8 %collective-permute-start = (f32[24,64]{1,0:T(8,128)S(1)}, f32[24,64]{1,0:T(8,128)S(1)}, u32[]{:S(2)}, u32[]{:S(2)}) collective-permute-start(f32[24,64]{1,0:T(8,128)S(1)} %constant_dynamic-slice_fusion), channel_id=1, source_target_pairs={{0,128},{128,0},{1,129},{129,1},{2,130},{130,2},{3,131},{131,3},{4... | collective-permute-start | bytes 18440 | tf_op jit(solution)/shard_map/ppermute | solution.py:21
  431.4 0.7 add_compare_fusion
  432.9 1.4 fusion.38
  (68 shorter events, 4.7 us)
Async XLA Ops:
  7.2 103.2 %copy-start = (f32[2,8,4,3072]{3,2,1,0:T(4,128)S(1)}, f32[2,8,4,3072]{3,2,1,0:T(4,128)}, u32[]{:S(2)}) copy-start(f32[2,8,4,3072]{3,2,1,0:T(4,128)} %param.23) | copy-start | bytes 2359300
  7.2 142.2 %all-gather.5.cloned.1.call-start = ((), (), s32[]{:S(2)}) async-start(), calls=%async_computation.2 | async-start | bytes 1327104 | tf_op jit(solution)/shard_map/all_gather | solution.py:113
  32.8 9.4 %copy-start.13 = (s32[1,96]{1,0:T(1,128)S(1)}, s32[1,96]{1,0:T(1,128)}, u32[]{:S(2)}) copy-start(s32[1,96]{1,0:T(1,128)} %param.19) | copy-start | bytes 1156
  64.6 11.8 %copy-start.14 = (s32[8]{0:T(128)S(1)}, s32[8]{0:T(128)}, u32[]{:S(2)}) copy-start(s32[8]{0:T(128)} %param.21) | copy-start | bytes 100
  64.6 13.1 %copy-start.9 = (bf16[1,1,48,1536]{3,2,1,0:T(8,128)(2,1)S(1)}, bf16[1,1,48,1536]{3,2,1,0:T(8,128)(2,1)}, u32[]{:S(2)}) copy-start(bf16[1,1,48,1536]{3,2,1,0:T(8,128)(2,1)} %param.15) | copy-start | bytes 442372
  77.7 7.8 %copy-start.11 = (pred[768]{0:T(1024)(128)(4,1)}, pred[768]{0:T(1024)(128)(4,1)S(1)}, u32[]{:S(2)}) copy-start(pred[768]{0:T(1024)(128)(4,1)S(1)} %iota_compare_fusion) | copy-start | bytes 2308
  84.0 1.8 copy-start.2
  84.0 1.8 copy-start.5
  86.4 1.3 copy-start.3
  93.0 11.8 %copy-start.10 = (f32[12,48]{1,0:T(8,128)S(1)}, f32[12,48]{1,0:T(8,128)}, u32[]{:S(2)}) copy-start(f32[12,48]{1,0:T(8,128)} %fusion.22) | copy-start | bytes 6916
  93.0 11.8 %copy-start.4 = (f32[12,768,48]{1,2,0:T(8,128)S(1)}, f32[12,768,48]{1,2,0:T(8,128)}, u32[]{:S(2)}) copy-start(f32[12,768,48]{1,2,0:T(8,128)} %copy-done.3) | copy-start | bytes 5308420
  93.0 11.8 %copy-start.8 = (f32[48,12,128]{2,0,1:T(8,128)S(1)}, f32[48,12,128]{2,0,1:T(8,128)}, u32[]{:S(2)}) copy-start(f32[48,12,128]{2,0,1:T(8,128)} %convolution_bitcast_fusion.1) | copy-start | bytes 884740
  93.0 11.8 %copy-start.12 = (pred[768]{0:T(1024)(128)(4,1)S(1)}, pred[768]{0:T(1024)(128)(4,1)}, u32[]{:S(2)}) copy-start(pred[768]{0:T(1024)(128)(4,1)} %copy-done.11) | copy-start | bytes 2308
  107.6 93.9 %copy-start.7 = (bf16[1,8,48,384]{3,2,1,0:T(8,128)(2,1)S(1)}, bf16[1,8,48,384]{3,2,1,0:T(8,128)(2,1)}, u32[]{:S(2)}) copy-start(bf16[1,8,48,384]{3,2,1,0:T(8,128)(2,1)} %param.22) | copy-start | bytes 884740
  108.3 93.2 %all-gather.7.cloned.1.call-start = ((), (), s32[]{:S(2)}) async-start(), calls=%async_computation.3 | async-start | bytes 1253376 | tf_op jit(solution)/shard_map/all_gather | solution.py:91
  109.0 175.9 %all-gather.11.cloned.1.call-start = ((), (), s32[]{:S(2)}) async-start(), calls=%async_computation.5 | async-start | bytes 10027008 | tf_op jit(solution)/shard_map/all_gather | solution.py:93
  109.8 257.9 %all-gather.9.cloned.1.call-start = ((), (), s32[]{:S(2)}) async-start(), calls=%async_computation.4 | async-start | bytes 10027008 | tf_op jit(solution)/shard_map/all_gather | solution.py:92
  205.7 64.0 %all-to-all-start = ((bf16[8,384,384]{1,2,0:T(8,128)(2,1)}), bf16[8,384,384]{1,2,0:T(8,128)(2,1)S(1)}, u32[]{:S(2)}, u32[]{:S(2)}) async-start(bf16[8,384,384]{1,2,0:T(8,128)(2,1)} %stack.15), calls=%async_computation | async-start | bytes 4718592 | tf_op jit(solution)/shard_map/all_to_all | solution.py:126
  212.5 212.8 %reduce-scatter.2.cloned.1.call-start = ((), (), s32[]{:S(2)}) async-start(), calls=%async_computation.6 | async-start | bytes 2654208 | tf_op jit(solution)/shard_map/reduce_scatter | solution.py:149
  386.4 38.9 %copy-start.6 = (bf16[3072,64]{0,1:T(8,128)(2,1)S(1)}, bf16[3072,64]{0,1:T(8,128)(2,1)}, u32[]{:S(2)}) copy-start(bf16[3072,64]{0,1:T(8,128)(2,1)} %param.27) | copy-start | bytes 1179652
  386.4 47.9 %copy-start.1 = (f32[2,8,4,3072]{3,2,1,0:T(4,128)S(1)}, f32[2,8,4,3072]{3,2,1,0:T(4,128)}, u32[]{:S(2)}) copy-start(f32[2,8,4,3072]{3,2,1,0:T(4,128)} %param.23) | copy-start | bytes 2359300
  426.6 6.2 %collective-permute-start = (f32[24,64]{1,0:T(8,128)S(1)}, f32[24,64]{1,0:T(8,128)S(1)}, u32[]{:S(2)}, u32[]{:S(2)}) collective-permute-start(f32[24,64]{1,0:T(8,128)S(1)} %constant_dynamic-slice_fusion), channel_id=1, source_target_pairs={{0,128},{128,0},{1,129},{129,1},{2,130},{130,2},{3,131},{131,3},{4... | collective-permute-start | bytes 18440 | tf_op jit(solution)/shard_map/ppermute | solution.py:21
Sparse Core Ops, SparseCore 0:
  108.4 40.9 all-gather.4
  151.8 49.5 all-gather.6
  203.9 80.9 all-gather.10
  287.2 80.4 all-gather.8
  386.5 38.7 reduce-scatter.1
